TPU v7x, 32 devices: a whole 2x2x4 slice. The times are simulated.
32 devices in a mesh: seq: 4 (over y, x), fsdp: 8 (over z, core).
Axes of the slice: x: 2, y: 2, z: 4, core: 2. Of those that a mesh axis runs over, the one named last changes fastest.
Arguments:
- tokens: bfloat16 [8, 1024, 768], P('fsdp', 'seq'), may hold values from -6 to 6
- cotangent: bfloat16 [8, 1024, 768], P('fsdp', 'seq'), may hold values from -6 to 6
- w_qkv: bfloat16 [768, 2304], P('fsdp'), may hold values from -0.21875 to 0.21875
- w_out: bfloat16 [768, 768], P('fsdp'), may hold values from -3.5 to 3.5
- w_gate: bfloat16 [768, 3072], P('fsdp'), may hold values from -0.21875 to 0.21875
- w_up: bfloat16 [768, 3072], P('fsdp'), may hold values from -0.21875 to 0.21875
- w_down: bfloat16 [3072, 768], P('fsdp'), may hold values from -0.21875 to 0.21875
- gain_one: bfloat16 [768], P('fsdp'), may hold values from 0.5 to 1.5
- bias_one: bfloat16 [768], P('fsdp'), may hold values from -1 to 1
- gain_two: bfloat16 [768], P('fsdp'), may hold values from 0.5 to 1.5
- bias_two: bfloat16 [768], P('fsdp'), may hold values from -1 to 1
- seq_lens: int32 [8], replicated, may hold values from 256 to 1024, as said below
- slot_seq: int32 [8], replicated, may hold values from 0 to 7, each once
Outputs:
- layer_out: bfloat16 [8, 1024, 768], P('fsdp', 'seq')
- grad_tokens: bfloat16 [8, 1024, 768], P('fsdp', 'seq')
- grad_qkv: float32 [768, 2304], P('fsdp')
- grad_out: float32 [768, 768], P('fsdp')
- grad_gate: float32 [768, 3072], P('fsdp')
- grad_up: float32 [768, 3072], P('fsdp')
- grad_down: float32 [3072, 768], P('fsdp')
- grad_gain_one: float32 [768], P('fsdp')
- grad_bias_one: float32 [768], P('fsdp')
- grad_gain_two: float32 [768], P('fsdp')
- grad_bias_two: float32 [768], P('fsdp')
- stream_rms: float32 [3], replicated
Inputs may be any that keep to these rules, and one draw needn't show every extreme that they name: `seq_lens`: one sequence has 1024 valid tokens and one has 256. `slot_seq`: each sequence is held by exactly one slot.
All inputs are finite; a program needn't handle non-finite values.
Results may differ from a plain program's by a relative error of at most 0.02.
Values may be sent and summed in bfloat16 or wider, within the bound.
No kernel may reach another device: no remote copies, remote signals or barrier semaphores. Data moves between devices by JAX's collectives and lax.ppermute only.
A program may use at most 128 MiB of HBM per device.

v0:
```python
import jax
import jax.numpy as jnp
from jax import lax
from jax.sharding import PartitionSpec as P

HD = 64


epsilon = 1e-12
rope_base = 1000.0
block_limit = 512


def rope_tables(positions, head_size):
    half_size = head_size // 2
    exponent = jnp.arange(half_size, dtype=jnp.float32) * (2.0 / head_size)
    frequency = jnp.power(jnp.float32(rope_base), -exponent)
    angles = positions[:, None] * frequency[None, :]
    cos_half = jnp.cos(angles)
    sin_half = jnp.sin(angles)
    return (
        jnp.concatenate([cos_half, cos_half], axis=-1),
        jnp.concatenate([sin_half, sin_half], axis=-1),
    )


def rotate(values_in, cos_table, sin_table):
    half_size = values_in.shape[-1] // 2
    turned = jnp.concatenate([-values_in[..., half_size:], values_in[..., :half_size]], axis=-1)
    return values_in * cos_table + turned * sin_table


def unrotate(grads_in, cos_table, sin_table):
    scaled = grads_in * sin_table
    half_size = grads_in.shape[-1] // 2
    turned = jnp.concatenate([scaled[..., half_size:], -scaled[..., :half_size]], axis=-1)
    return grads_in * cos_table + turned


def lookup(table, position):
    marks = jnp.arange(table.shape[0], dtype=jnp.int32) == position
    return jnp.sum(jnp.where(marks, table, 0))


def layer_norm(stream, gain_vec, bias_vec):
    average = jnp.mean(stream, axis=-1, keepdims=True)
    centred = stream - average
    variance = jnp.mean(centred * centred, axis=-1, keepdims=True)
    inverse = lax.rsqrt(variance + epsilon)
    normal = centred * inverse
    return (normal * gain_vec + bias_vec, normal, inverse)


def norm_back(grad_rows, normal, inverse, gain_vec):
    scaled = grad_rows * gain_vec
    first_mean = jnp.mean(scaled, axis=-1, keepdims=True)
    second_mean = jnp.mean(scaled * normal, axis=-1, keepdims=True)
    grad_in = (scaled - first_mean - normal * second_mean) * inverse
    return (grad_in, jnp.sum(grad_rows * normal, axis=0), jnp.sum(grad_rows, axis=0))


def gather_weights(shards):
    gathered = (
        lax.all_gather(shards[0], "fsdp", axis=0, tiled=True),
        lax.all_gather(shards[1], "fsdp", axis=0, tiled=True),
        lax.all_gather(shards[2], "fsdp", axis=0, tiled=True),
        lax.all_gather(shards[3], "fsdp", axis=0, tiled=True),
        lax.all_gather(shards[4], "fsdp", axis=0, tiled=True),
        lax.all_gather(shards[5], "fsdp", axis=0, tiled=True),
        lax.all_gather(shards[6], "fsdp", axis=0, tiled=True),
        lax.all_gather(shards[7], "fsdp", axis=0, tiled=True),
        lax.all_gather(shards[8], "fsdp", axis=0, tiled=True),
    )
    return list(gathered)


def reduce_grads(grads_all):
    owned = (
        lax.psum_scatter(grads_all[0], "fsdp", scatter_dimension=0, tiled=True),
        lax.psum_scatter(grads_all[1], "fsdp", scatter_dimension=0, tiled=True),
        lax.psum_scatter(grads_all[2], "fsdp", scatter_dimension=0, tiled=True),
        lax.psum_scatter(grads_all[3], "fsdp", scatter_dimension=0, tiled=True),
        lax.psum_scatter(grads_all[4], "fsdp", scatter_dimension=0, tiled=True),
        lax.psum_scatter(grads_all[5], "fsdp", scatter_dimension=0, tiled=True),
        lax.psum_scatter(grads_all[6], "fsdp", scatter_dimension=0, tiled=True),
        lax.psum_scatter(grads_all[7], "fsdp", scatter_dimension=0, tiled=True),
        lax.psum_scatter(grads_all[8], "fsdp", scatter_dimension=0, tiled=True),
    )
    split = (
        lax.psum_scatter(
            owned[0].astype(jnp.bfloat16), "seq", scatter_dimension=0, tiled=True
        ).astype(jnp.float32),
        lax.psum_scatter(
            owned[1].astype(jnp.bfloat16), "seq", scatter_dimension=0, tiled=True
        ).astype(jnp.float32),
        lax.psum_scatter(
            owned[2].astype(jnp.bfloat16), "seq", scatter_dimension=0, tiled=True
        ).astype(jnp.float32),
        lax.psum_scatter(
            owned[3].astype(jnp.bfloat16), "seq", scatter_dimension=0, tiled=True
        ).astype(jnp.float32),
        lax.psum_scatter(
            owned[4].astype(jnp.bfloat16), "seq", scatter_dimension=0, tiled=True
        ).astype(jnp.float32),
        lax.psum_scatter(
            owned[5].astype(jnp.bfloat16), "seq", scatter_dimension=0, tiled=True
        ).astype(jnp.float32),
        lax.psum_scatter(
            owned[6].astype(jnp.bfloat16), "seq", scatter_dimension=0, tiled=True
        ).astype(jnp.float32),
        lax.psum_scatter(
            owned[7].astype(jnp.bfloat16), "seq", scatter_dimension=0, tiled=True
        ).astype(jnp.float32),
        lax.psum_scatter(
            owned[8].astype(jnp.bfloat16), "seq", scatter_dimension=0, tiled=True
        ).astype(jnp.float32),
    )
    return (
        lax.all_gather(split[0].astype(jnp.bfloat16), "seq", axis=0, tiled=True).astype(
            jnp.float32
        ),
        lax.all_gather(split[1].astype(jnp.bfloat16), "seq", axis=0, tiled=True).astype(
            jnp.float32
        ),
        lax.all_gather(split[2].astype(jnp.bfloat16), "seq", axis=0, tiled=True).astype(
            jnp.float32
        ),
        lax.all_gather(split[3].astype(jnp.bfloat16), "seq", axis=0, tiled=True).astype(
            jnp.float32
        ),
        lax.all_gather(split[4].astype(jnp.bfloat16), "seq", axis=0, tiled=True).astype(
            jnp.float32
        ),
        lax.all_gather(split[5].astype(jnp.bfloat16), "seq", axis=0, tiled=True).astype(
            jnp.float32
        ),
        lax.all_gather(split[6].astype(jnp.bfloat16), "seq", axis=0, tiled=True).astype(
            jnp.float32
        ),
        lax.all_gather(split[7].astype(jnp.bfloat16), "seq", axis=0, tiled=True).astype(
            jnp.float32
        ),
        lax.all_gather(split[8].astype(jnp.bfloat16), "seq", axis=0, tiled=True).astype(
            jnp.float32
        ),
    )


def masked_scores(query_block, key_rows, key_mask, score_scale):
    scores = (
        jnp.einsum("qhe,khe->hqk", query_block, key_rows, preferred_element_type=jnp.float32)
        * score_scale
    )
    return jnp.where(key_mask[None, None, :], scores, -1e30)


def attend(queries, key_rows, values, key_mask, block_count):
    seqlen, head_count, head_size = queries.shape
    block_rows = min(block_limit, seqlen)
    score_scale = head_size ** (-0.5)

    def one_block(block_index, loop_state):
        out_rows, log_totals = loop_state
        offset = block_index * block_rows
        query_block = lax.dynamic_slice_in_dim(queries, offset, block_rows, 0)
        scores = masked_scores(query_block, key_rows, key_mask, score_scale)
        row_max = jnp.max(scores, axis=-1, keepdims=True)
        raised = jnp.exp(scores - row_max)
        row_total = jnp.sum(raised, axis=-1, keepdims=True)
        attn_probs = (raised / row_total).astype(jnp.bfloat16)
        attended = jnp.einsum(
            "hqk,khe->qhe", attn_probs, values, preferred_element_type=jnp.float32
        )
        attended = attended.astype(jnp.bfloat16).reshape(block_rows, head_count * head_size)
        out_rows = lax.dynamic_update_slice_in_dim(out_rows, attended, offset, 0)
        log_totals = lax.dynamic_update_slice_in_dim(
            log_totals, (row_max + jnp.log(row_total))[..., 0], offset, 1
        )
        return (out_rows, log_totals)

    initial = (
        jnp.zeros((seqlen, head_count * head_size), jnp.bfloat16),
        jnp.zeros((head_count, seqlen), jnp.float32),
    )
    return lax.fori_loop(0, block_count, one_block, initial)


def attend_back(queries, key_rows, values, grad_heads, log_totals, key_mask, block_count):
    seqlen, head_count, head_size = queries.shape
    block_rows = min(block_limit, seqlen)
    score_scale = head_size ** (-0.5)
    grad_shaped = grad_heads.reshape(seqlen, head_count, head_size)

    def one_block(block_index, loop_state):
        grad_query, grad_key, grad_value = loop_state
        offset = block_index * block_rows
        query_block = lax.dynamic_slice_in_dim(queries, offset, block_rows, 0)
        grad_block = lax.dynamic_slice_in_dim(grad_shaped, offset, block_rows, 0)
        log_block = lax.dynamic_slice_in_dim(log_totals, offset, block_rows, 1)
        scores = masked_scores(query_block, key_rows, key_mask, score_scale)
        attn_probs = jnp.exp(scores - log_block[..., None])
        grad_probs = jnp.einsum(
            "qhe,khe->hqk", grad_block, values, preferred_element_type=jnp.float32
        )
        row_dot = jnp.sum(attn_probs * grad_probs, axis=-1, keepdims=True)
        grad_scores = (attn_probs * (grad_probs - row_dot)).astype(jnp.bfloat16)
        query_part = (
            jnp.einsum("hqk,khe->qhe", grad_scores, key_rows, preferred_element_type=jnp.float32)
            * score_scale
        )
        grad_query = lax.dynamic_update_slice_in_dim(
            grad_query, query_part.astype(jnp.bfloat16), offset, 0
        )
        grad_key = (
            grad_key
            + jnp.einsum(
                "hqk,qhe->khe", grad_scores, query_block, preferred_element_type=jnp.float32
            )
            * score_scale
        )
        grad_value = grad_value + jnp.einsum(
            "hqk,qhe->khe",
            attn_probs.astype(jnp.bfloat16),
            grad_block,
            preferred_element_type=jnp.float32,
        )
        return (grad_query, grad_key, grad_value)

    initial = (
        jnp.zeros((seqlen, head_count, head_size), jnp.bfloat16),
        jnp.zeros((seqlen, head_count, head_size), jnp.float32),
        jnp.zeros((seqlen, head_count, head_size), jnp.float32),
    )
    grad_query, grad_key, grad_value = lax.fori_loop(0, block_count, one_block, initial)
    return (grad_query, grad_key.astype(jnp.bfloat16), grad_value.astype(jnp.bfloat16))


def body(
    tokens,
    cotangent,
    w_qkv,
    w_out,
    w_gate,
    w_up,
    w_down,
    gain_one,
    bias_one,
    gain_two,
    bias_two,
    seq_lens,
    slot_seq,
):
    seq_parts = lax.axis_size("seq")
    tok_rows = tokens.shape[1]
    model_width = tokens.shape[2]
    head_size = HD
    local_heads = model_width // head_size // seq_parts
    group_width = 3 * local_heads * head_size
    seqlen = tok_rows * seq_parts
    block_rows = min(block_limit, seqlen)
    stream_in = tokens[0]
    length = lookup(seq_lens, lookup(slot_seq, lax.axis_index("fsdp")))
    positions = lax.axis_index("seq") * tok_rows + jnp.arange(tok_rows, dtype=jnp.int32)
    keep_mask = (positions < length).astype(jnp.float32)
    column = keep_mask[:, None]
    key_mask = jnp.arange(seqlen, dtype=jnp.int32) < length
    block_count = seqlen // block_rows
    gathered = gather_weights(
        (w_qkv, w_out, w_gate, w_up, w_down, gain_one, bias_one, gain_two, bias_two)
    )
    full_qkv, full_out, full_gate, full_up, full_down = (
        gathered[0],
        gathered[1],
        gathered[2],
        gathered[3],
        gathered[4],
    )
    gain_first = gathered[5].astype(jnp.float32)
    bias_first = gathered[6].astype(jnp.float32)
    gain_second = gathered[7].astype(jnp.float32)
    bias_second = gathered[8].astype(jnp.float32)
    mixed_qkv = (
        full_qkv.reshape(model_width, 3, seq_parts, local_heads * head_size)
        .transpose(0, 2, 1, 3)
        .reshape(model_width, 3 * model_width)
    )
    projected = jnp.dot(stream_in, mixed_qkv, preferred_element_type=jnp.float32).reshape(
        tok_rows, seq_parts, 3, local_heads, head_size
    )
    cos_table, sin_table = rope_tables(positions.astype(jnp.float32), head_size)
    cos_table = cos_table[:, None, None, :]
    sin_table = sin_table[:, None, None, :]
    packed = jnp.stack(
        [
            rotate(projected[:, :, 0], cos_table, sin_table),
            rotate(projected[:, :, 1], cos_table, sin_table),
            projected[:, :, 2],
        ],
        axis=2,
    )
    packed = packed.astype(jnp.bfloat16).reshape(tok_rows, seq_parts * group_width)
    received = lax.all_to_all(packed, "seq", split_axis=1, concat_axis=0, tiled=True).reshape(
        seqlen, 3, local_heads, head_size
    )
    queries = received[:, 0]
    key_rows = received[:, 1]
    values = received[:, 2]
    head_out, log_totals = attend(queries, key_rows, values, key_mask, block_count)
    head_mix = lax.all_to_all(head_out, "seq", split_axis=0, concat_axis=1, tiled=True)
    branch_attn = jnp.dot(head_mix, full_out, preferred_element_type=jnp.float32)
    stream_float = stream_in.astype(jnp.float32)
    normed_float, normal_one, inverse_one = layer_norm(
        stream_float + branch_attn, gain_first, bias_first
    )
    normed_one = normed_float.astype(jnp.bfloat16)
    gate_proj = jnp.dot(normed_one, full_gate, preferred_element_type=jnp.float32)
    up_proj = jnp.dot(normed_one, full_up, preferred_element_type=jnp.float32)
    inner_act = (jax.nn.silu(gate_proj) * up_proj).astype(jnp.bfloat16)
    branch_ffn = jnp.dot(inner_act, full_down, preferred_element_type=jnp.float32)
    out_float, normal_two, inverse_two = layer_norm(
        normed_one.astype(jnp.float32) + branch_ffn, gain_second, bias_second
    )
    layer_out = (out_float * column).astype(jnp.bfloat16)
    totals = lax.psum(
        (
            jnp.sum(column * stream_float * stream_float),
            jnp.sum(column * branch_attn * branch_attn),
            jnp.sum(column * branch_ffn * branch_ffn),
        ),
        ("seq", "fsdp"),
    )
    denominator = jnp.sum(seq_lens).astype(jnp.float32) * model_width
    stream_rms = jnp.sqrt(jnp.stack([totals[0], totals[1], totals[2]]) / denominator)
    grad_rows = cotangent[0].astype(jnp.float32) * column
    grad_two, gain_two_grad, bias_two_grad = norm_back(
        grad_rows, normal_two, inverse_two, gain_second
    )
    grad_ffn = grad_two.astype(jnp.bfloat16)
    down_grad = jnp.einsum("tf,td->fd", inner_act, grad_ffn, preferred_element_type=jnp.float32)
    grad_inner = jnp.einsum("td,fd->tf", grad_ffn, full_down, preferred_element_type=jnp.float32)
    sigmoid_gate = jax.nn.sigmoid(gate_proj)
    grad_gate_rows = (
        grad_inner * up_proj * sigmoid_gate * (1.0 + gate_proj * (1.0 - sigmoid_gate))
    ).astype(jnp.bfloat16)
    grad_up_rows = (grad_inner * gate_proj * sigmoid_gate).astype(jnp.bfloat16)
    gate_grad = jnp.einsum(
        "td,tf->df", normed_one, grad_gate_rows, preferred_element_type=jnp.float32
    )
    up_grad = jnp.einsum("td,tf->df", normed_one, grad_up_rows, preferred_element_type=jnp.float32)
    grad_normed = jnp.einsum(
        "tf,df->td", grad_gate_rows, full_gate, preferred_element_type=jnp.float32
    )
    grad_normed = (
        grad_normed
        + jnp.einsum("tf,df->td", grad_up_rows, full_up, preferred_element_type=jnp.float32)
        + grad_two
    )
    grad_one, gain_one_grad, bias_one_grad = norm_back(
        grad_normed, normal_one, inverse_one, gain_first
    )
    grad_attn = grad_one.astype(jnp.bfloat16)
    out_grad = jnp.einsum("td,te->de", head_mix, grad_attn, preferred_element_type=jnp.float32)
    grad_mix = jnp.einsum(
        "te,de->td", grad_attn, full_out, preferred_element_type=jnp.float32
    ).astype(jnp.bfloat16)
    grad_heads = lax.all_to_all(grad_mix, "seq", split_axis=1, concat_axis=0, tiled=True)
    grad_query, grad_key, grad_value = attend_back(
        queries, key_rows, values, grad_heads, log_totals, key_mask, block_count
    )
    grad_packed = jnp.stack([grad_query, grad_key, grad_value], axis=1).reshape(seqlen, group_width)
    grad_back = lax.all_to_all(grad_packed, "seq", split_axis=0, concat_axis=1, tiled=True).reshape(
        tok_rows, seq_parts, 3, local_heads, head_size
    )
    grad_proj = jnp.stack(
        [
            unrotate(grad_back[:, :, 0].astype(jnp.float32), cos_table, sin_table),
            unrotate(grad_back[:, :, 1].astype(jnp.float32), cos_table, sin_table),
            grad_back[:, :, 2].astype(jnp.float32),
        ],
        axis=2,
    )
    grad_proj = grad_proj.astype(jnp.bfloat16).reshape(tok_rows, 3 * model_width)
    mixed_grad = jnp.einsum("td,tc->dc", stream_in, grad_proj, preferred_element_type=jnp.float32)
    qkv_grad = (
        mixed_grad.reshape(model_width, seq_parts, 3, local_heads * head_size)
        .transpose(0, 2, 1, 3)
        .reshape(model_width, 3 * model_width)
    )
    grad_tokens = (
        jnp.einsum("tc,dc->td", grad_proj, mixed_qkv, preferred_element_type=jnp.float32) + grad_one
    ).astype(jnp.bfloat16)
    owned = reduce_grads(
        (
            qkv_grad,
            out_grad,
            gate_grad,
            up_grad,
            down_grad,
            gain_one_grad,
            bias_one_grad,
            gain_two_grad,
            bias_two_grad,
        )
    )
    return (
        layer_out[None],
        grad_tokens[None],
        owned[0],
        owned[1],
        owned[2],
        owned[3],
        owned[4],
        owned[5],
        owned[6],
        owned[7],
        owned[8],
        stream_rms,
    )


def solution(mesh):
    placed = (
        P("fsdp", "seq", None),
        P("fsdp", "seq", None),
        P("fsdp", None),
        P("fsdp", None),
        P("fsdp", None),
        P("fsdp", None),
        P("fsdp", None),
        P("fsdp"),
        P("fsdp"),
        P("fsdp"),
        P("fsdp"),
        P(),
        P(),
    )
    return jax.shard_map(
        body,
        mesh=mesh,
        in_specs=placed,
        out_specs=(
            P("fsdp", "seq", None),
            P("fsdp", "seq", None),
            P("fsdp", None),
            P("fsdp", None),
            P("fsdp", None),
            P("fsdp", None),
            P("fsdp", None),
            P("fsdp"),
            P("fsdp"),
            P("fsdp"),
            P("fsdp"),
            P(),
        ),
        check_vma=False,
    )
```

profile of v0, /device:TPU:8, one launch (start us, length us, event | category | flops | bytes accessed | tf_op | source)
XLA Modules:
  0.0 881.8 jit_solution(7419135295080579601)
XLA Ops:
  10.9 40.4 %all-gather.6.cloned.1.call-done = bf16[768,2304]{1,0:T(8,128)(2,1)} async-done(((bf16[96,2304]{1,0:T(8,128)(2,1)}), bf16[768,2304]{1,0:T(8,128)(2,1)}) %all-gather.6.cloned.1.call-update) | async-done | bytes 3538960 | tf_op jit(solution)/shard_map/all_gather | solution.py:64
  66.5 13.1 %all-to-all-done = bf16[256,4,576]{0,2,1:T(8,128)(2,1)S(1)} async-done(((bf16[256,4,576]{0,2,1:T(8,128)(2,1)}), bf16[256,4,576]{0,2,1:T(8,128)(2,1)S(1)}, u32[]{:S(2)}, u32[]{:S(2)}) %all-to-all-start) | async-done | bytes 1179680 | tf_op jit(solution)/shard_map/all_to_all | solution.py:302
  81.6 10.9 %while.34 = (s32[]{:T(128)}, bf16[1024,192]{0,1:T(8,128)(2,1)S(1)}, f32[3,1024]{1,0:T(4,128)S(1)}, bf16[1024,3,64]{0,2,1:T(8,128)(2,1)S(1)}, bf16[1024,3,64]{0,2...) while((s32[]{:T(128)}, bf16[1024,192]{0,1:T(8,128)(2,1)S(1)}, ...), condition=%wide.region_5.6_spmd.clone, body=%wide.region_2.5_spmd.clone.sunk | while | flops 421625344 | bytes 20506796 | solution.py:185
  99.1 15.0 %all-reduce.22 = (bf16[768]{0:T(1024)(128)(2,1)S(1)}, bf16[768]{0:T(1024)(128)(2,1)S(1)}, bf16[768]{0:T(1024)(128)(2,1)S(1)}, bf16[768]{0:T(1024)(128)(2,1)S(1)}) all-reduce(bf16[768]{0:T(1024)(128)(2,1)S(1)} %dynamic-update-slice.1, bf16[768]{0:T(1024)(128)(2,1)S(1)} %dynamic-update-slice, ...), channel_id=1, replica_groups=mesh['seq'=4,'fsdp'=8] {'fsdp'}, use_global_device_ids=true, to_apply=%add.1 | all-reduce | flops 3072 | bytes 12288
  118.0 9.1 %all-gather.10.cloned.1.call-done = bf16[768,3072]{1,0:T(8,128)(2,1)} async-done(((bf16[96,3072]{1,0:T(8,128)(2,1)}), bf16[768,3072]{1,0:T(8,128)(2,1)}) %all-gather.10.cloned.1.call-update) | async-done | bytes 4718608 | tf_op jit(solution)/shard_map/all_gather | solution.py:66
  132.4 46.1 %all-gather.12.cloned.1.call-done = bf16[768,3072]{1,0:T(8,128)(2,1)} async-done(((bf16[96,3072]{1,0:T(8,128)(2,1)}), bf16[768,3072]{1,0:T(8,128)(2,1)}) %all-gather.12.cloned.1.call-update) | async-done | bytes 4718608 | tf_op jit(solution)/shard_map/all_gather | solution.py:67
  185.7 44.3 %all-gather.14.cloned.1.call-done = bf16[3072,768]{1,0:T(8,128)(2,1)} async-done(((bf16[384,768]{1,0:T(8,128)(2,1)}), bf16[3072,768]{1,0:T(8,128)(2,1)}) %all-gather.14.cloned.1.call-update) | async-done | bytes 4718608 | tf_op jit(solution)/shard_map/all_gather | solution.py:68
  260.7 27.6 %while.35 = (s32[]{:T(128)}, bf16[1024,3,64]{0,2,1:T(8,128)(2,1)}, f32[1024,3,64]{0,2,1:T(8,128)}, f32[1024,3,64]{0,2,1:T(8,128)}, bf16[1024,3,64]{0,2,1:T(8,128...) while((s32[]{:T(128)}, bf16[1024,3,64]{0,2,1:T(8,128)(2,1)}, ...), condition=%wide.region_16.17_spmd.clone, body=%wide.region_14.16_spmd.clone.sunk | while | flops 1031405056 | bytes 112411136 | solution.py:234
  292.9 17.7 %all_to_all.64 = bf16[4,256,576]{1,2,0:T(8,128)(2,1)S(1)} all-to-all(bf16[4,256,576]{1,2,0:T(8,128)(2,1)S(1)} %copy.71), channel_id=1, replica_groups=mesh['seq'=4,'fsdp'=8] {'seq'}, dimensions={0} | all-to-all | bytes 2359296 | tf_op jit(solution)/shard_map/all_to_all | solution.py:371
  346.7 51.5 %reduce-scatter.29.cloned.1.call-done = f32[96,2304]{1,0:T(8,128)} async-done(((f32[768,2304]{1,0:T(8,128)}), f32[96,2304]{1,0:T(8,128)}) %reduce-scatter.29.cloned.1.call-update) | async-done | bytes 884752
  400.5 97.9 %reduce-scatter.25.cloned.1.call-done = f32[384,768]{1,0:T(8,128)} async-done(((f32[3072,768]{1,0:T(8,128)}), f32[384,768]{1,0:T(8,128)}) %reduce-scatter.25.cloned.1.call-update) | async-done | bytes 1179664 | tf_op jit(solution)/shard_map/reduce_scatter | solution.py:83
  500.7 98.0 %reduce-scatter.21.cloned.1.call-done = f32[96,3072]{1,0:T(8,128)} async-done(((f32[768,3072]{1,0:T(8,128)}), f32[96,3072]{1,0:T(8,128)}) %reduce-scatter.21.cloned.1.call-update) | async-done | bytes 1179664 | tf_op jit(solution)/shard_map/reduce_scatter | solution.py:81
  603.5 43.7 %all-reduce.20 = (f32[1]{0:T(128)}, f32[1]{0:T(128)}, f32[1]{0:T(128)}) all-reduce(f32[1]{0:T(128)} %bitcast.53, f32[1]{0:T(128)} %bitcast.52, f32[1]{0:T(128)} %bitcast.51), channel_id=1, replica_groups=mesh['seq'=4,'fsdp'=8] {'seq','fsdp'}, use_global_device_ids=true, to_apply=%region_44.45 | all-reduce | flops 3 | bytes 24 | tf_op jit(solution)/shard_map/psum | solution.py:324
  647.2 24.5 %all-reduce.21 = (bf16[768]{0:T(1024)(128)(2,1)}, bf16[768]{0:T(1024)(128)(2,1)}, bf16[768]{0:T(1024)(128)(2,1)}, bf16[768]{0:T(1024)(128)(2,1)}) all-reduce(f32[768]{0:T(1024)S(1)} %copy-done.46, f32[768]{0:T(1024)S(1)} %copy-done.47, f32[768]{0:T(1024)S(1)} %copy-done.35, ...), channel_id=12, replica_groups=mesh['seq'=4,'fsdp'=8] {'fsdp'}, use_global_device_ids=true, to_apply=%region_28.29.clone | all-reduce | flops 3072 | bytes 18432
  674.7 9.3 %all-reduce.24 = (bf16[96]{0:T(256)(128)(2,1)}, bf16[96]{0:T(256)(128)(2,1)}, bf16[96]{0:T(256)(128)(2,1)}, bf16[96]{0:T(256)(128)(2,1)}) all-reduce(bf16[96]{0:T(256)(128)(2,1)S(1)} %dynamic-slice.40, bf16[96]{0:T(256)(128)(2,1)S(1)} %dynamic-slice.39, ...), channel_id=13, replica_groups=mesh['seq'=4,'fsdp'=8] {'seq'}, use_global_device_ids=true, to_apply=%region_29.30.clone | all-reduce | flops 384 | bytes 1536
  710.4 18.2 %reduce-scatter.31.cloned.1.call-done = bf16[24,768]{1,0:T(8,128)(2,1)} async-done(((bf16[96,768]{1,0:T(8,128)(2,1)}), bf16[24,768]{1,0:T(8,128)(2,1)}) %reduce-scatter.31.cloned.1.call-update) | async-done | bytes 36880
  738.0 40.2 %all-reduce.27.cloned.1.call-done = bf16[96,2304]{0,1:T(8,128)(2,1)} async-done(((bf16[96,2304]{0,1:T(8,128)(2,1)}), bf16[96,2304]{0,1:T(8,128)(2,1)}) %all-reduce.27.cloned.1.call-update) | async-done | bytes 442384
  779.6 9.9 %all_gather.63 = bf16[96,2304]{1,0:T(8,128)(2,1)S(1)} all-gather(bf16[24,2304]{1,0:T(8,128)(2,1)S(1)} %copy.77), channel_id=1, replica_groups=mesh['seq'=4,'fsdp'=8] {'seq'}, dimensions={0}, use_global_device_ids=true | all-gather | bytes 552960 | tf_op jit(solution)/shard_map/all_gather | solution.py:119
  790.5 16.0 %reduce-scatter.27.cloned.1.call-done = bf16[96,768]{1,0:T(8,128)(2,1)} async-done(((bf16[384,768]{1,0:T(8,128)(2,1)}), bf16[96,768]{1,0:T(8,128)(2,1)}) %reduce-scatter.27.cloned.1.call-update) | async-done | bytes 147472 | tf_op jit(solution)/shard_map/reduce_scatter | solution.py:102
  806.5 10.2 %all_gather.67 = bf16[384,768]{1,0:T(8,128)(2,1)S(1)} all-gather(bf16[96,768]{1,0:T(8,128)(2,1)} %reduce-scatter.27.cloned.1.call-done), channel_id=1, replica_groups=mesh['seq'=4,'fsdp'=8] {'seq'}, dimensions={0}, use_global_device_ids=true | all-gather | bytes 737280 | tf_op jit(solution)/shard_map/all_gather | solution.py:131
  817.8 17.4 %reduce-scatter.33.cloned.1.call-done = bf16[24,3072]{1,0:T(8,128)(2,1)} async-done(((bf16[96,3072]{1,0:T(8,128)(2,1)}), bf16[24,3072]{1,0:T(8,128)(2,1)}) %reduce-scatter.33.cloned.1.call-update) | async-done | bytes 147472
  835.2 10.2 %all_gather.65 = bf16[96,3072]{1,0:T(8,128)(2,1)S(1)} all-gather(bf16[24,3072]{1,0:T(8,128)(2,1)} %reduce-scatter.33.cloned.1.call-done), channel_id=1, replica_groups=mesh['seq'=4,'fsdp'=8] {'seq'}, dimensions={0}, use_global_device_ids=true | all-gather | bytes 737280 | tf_op jit(solution)/shard_map/all_gather | solution.py:125
  846.6 16.8 %reduce-scatter.35.cloned.1.call-done = bf16[24,3072]{1,0:T(8,128)(2,1)} async-done(((bf16[96,3072]{1,0:T(8,128)(2,1)}), bf16[24,3072]{1,0:T(8,128)(2,1)}) %reduce-scatter.35.cloned.1.call-update) | async-done | bytes 147472
  863.4 10.2 %all_gather.66 = bf16[96,3072]{1,0:T(8,128)(2,1)S(1)} all-gather(bf16[24,3072]{1,0:T(8,128)(2,1)} %reduce-scatter.35.cloned.1.call-done), channel_id=1, replica_groups=mesh['seq'=4,'fsdp'=8] {'seq'}, dimensions={0}, use_global_device_ids=true | all-gather | bytes 737280 | tf_op jit(solution)/shard_map/all_gather | solution.py:128
  (331 shorter events, 202.8 us)
Async XLA Ops:
  7.2 44.1 %all-gather.6.cloned.1.call-start = ((), (), s32[]{:S(2)}) async-start(), calls=%async_computation.13 | async-start | bytes 3981312 | tf_op jit(solution)/shard_map/all_gather | solution.py:64
  7.9 106.9 %all-gather.8.cloned.1.call-start = ((), (), s32[]{:S(2)}) async-start(), calls=%async_computation.14 | async-start | bytes 1327104 | tf_op jit(solution)/shard_map/all_gather | solution.py:65
  8.7 118.4 %all-gather.10.cloned.1.call-start = ((), (), s32[]{:S(2)}) async-start(), calls=%async_computation.15 | async-start | bytes 5308416 | tf_op jit(solution)/shard_map/all_gather | solution.py:66
  9.4 169.2 %all-gather.12.cloned.1.call-start = ((), (), s32[]{:S(2)}) async-start(), calls=%async_computation.16 | async-start | bytes 5308416 | tf_op jit(solution)/shard_map/all_gather | solution.py:67
  60.4 19.2 %all-to-all-start = ((bf16[256,4,576]{0,2,1:T(8,128)(2,1)}), bf16[256,4,576]{0,2,1:T(8,128)(2,1)S(1)}, u32[]{:S(2)}, u32[]{:S(2)}) async-start(bf16[256,4,576]{0,2,1:T(8,128)(2,1)} %bitcast.16), calls=%async_computation | async-start | bytes 2359296 | tf_op jit(solution)/shard_map/all_to_all | solution.py:302
  64.0 166.0 %all-gather.14.cloned.1.call-start = ((), (), s32[]{:S(2)}) async-start(), calls=%async_computation.17 | async-start | bytes 5308416 | tf_op jit(solution)/shard_map/all_gather | solution.py:68
  93.3 21.5 %all-to-all-start.1 = ((bf16[4,256,192]{1,2,0:T(8,128)(2,1)}), bf16[4,256,192]{1,2,0:T(8,128)(2,1)S(1)}, u32[]{:S(2)}, u32[]{:S(2)}) async-start(bf16[4,256,192]{1,2,0:T(8,128)(2,1)} %bitcast.196), calls=%async_computation.1 | async-start | bytes 786432 | tf_op jit(solution)/shard_map/all_to_all | solution.py:309
  114.8 129.5 %copy-start.38 = (f32[256]{0:T(256)}, f32[256]{0:T(256)S(1)}, u32[]{:S(2)}) copy-start(f32[256]{0:T(256)S(1)} %compare_convert_fusion) | copy-start | bytes 3076
  248.6 10.7 %all-to-all-start.2 = ((bf16[256,4,192]{0,2,1:T(8,128)(2,1)}), bf16[256,4,192]{0,2,1:T(8,128)(2,1)S(1)}, u32[]{:S(2)}, u32[]{:S(2)}) async-start(bf16[256,4,192]{0,2,1:T(8,128)(2,1)} %bitcast.26), calls=%async_computation.2 | async-start | bytes 786432 | tf_op jit(solution)/shard_map/all_to_all | solution.py:366
  252.2 92.7 %reduce-scatter.19.cloned.1.call-start = ((), (), s32[]{:S(2)}) async-start(), calls=%async_computation.18 | async-start | bytes 2654208 | tf_op jit(solution)/shard_map/reduce_scatter | solution.py:80
  254.1 144.1 %reduce-scatter.29.cloned.1.call-start = ((), (), s32[]{:S(2)}) async-start(), calls=%async_computation.23 | async-start | bytes 7962624
  324.6 173.8 %reduce-scatter.25.cloned.1.call-start = ((), (), s32[]{:S(2)}) async-start(), calls=%async_computation.21 | async-start | bytes 10616832 | tf_op jit(solution)/shard_map/reduce_scatter | solution.py:83
  331.8 266.9 %reduce-scatter.21.cloned.1.call-start = ((), (), s32[]{:S(2)}) async-start(), calls=%async_computation.19 | async-start | bytes 10616832 | tf_op jit(solution)/shard_map/reduce_scatter | solution.py:81
  338.3 364.1 %reduce-scatter.23.cloned.1.call-start = ((), (), s32[]{:S(2)}) async-start(), calls=%async_computation.20 | async-start | bytes 10616832 | tf_op jit(solution)/shard_map/reduce_scatter | solution.py:82
  344.9 383.8 %reduce-scatter.31.cloned.1.call-start = ((), (), s32[]{:S(2)}) async-start(), calls=%async_computation.25 | async-start | bytes 184320
  346.6 300.6 %copy-start.34 = (f32[768]{0:T(1024)S(1)}, f32[768]{0:T(1024)}, u32[]{:S(2)}) copy-start(f32[768]{0:T(1024)} %get-tuple-element.401) | copy-start | bytes 9220
  346.6 300.6 %copy-start.35 = (f32[768]{0:T(1024)S(1)}, f32[768]{0:T(1024)}, u32[]{:S(2)}) copy-start(f32[768]{0:T(1024)} %get-tuple-element.404) | copy-start | bytes 9220
  346.6 300.6 %copy-start.46 = (f32[768]{0:T(1024)S(1)}, f32[768]{0:T(1024)}, u32[]{:S(2)}) copy-start(f32[768]{0:T(1024)} %get-tuple-element.390) | copy-start | bytes 9220
  346.6 300.6 %copy-start.47 = (f32[768]{0:T(1024)S(1)}, f32[768]{0:T(1024)}, u32[]{:S(2)}) copy-start(f32[768]{0:T(1024)} %get-tuple-element.395) | copy-start | bytes 9220
  346.7 431.5 %all-reduce.27.cloned.1.call-start = ((), (), s32[]{:S(2)}) async-start(), calls=%async_computation.24 | async-start | bytes 1179648
  400.5 406.0 %reduce-scatter.27.cloned.1.call-start = ((), (), s32[]{:S(2)}) async-start(), calls=%async_computation.22 | async-start | bytes 737280 | tf_op jit(solution)/shard_map/reduce_scatter | solution.py:102
  500.6 206.5 %copy-start.7 = (bf16[768,4,3,192]{0,3,2,1:T(8,128)(2,1)S(1)}, bf16[768,4,3,192]{0,3,2,1:T(8,128)(2,1)}, u32[]{:S(2)}) copy-start(bf16[768,4,3,192]{0,3,2,1:T(8,128)(2,1)} %copy-done.6) | copy-start | bytes 10616836
  500.6 334.6 %reduce-scatter.33.cloned.1.call-start = ((), (), s32[]{:S(2)}) async-start(), calls=%async_computation.26 | async-start | bytes 737280
  600.8 262.6 %reduce-scatter.35.cloned.1.call-start = ((), (), s32[]{:S(2)}) async-start(), calls=%async_computation.27 | async-start | bytes 737280
  (67 other events, 483.6 us)
Sparse Core Ops, SparseCore 0:
  9.6 41.5 all-gather.5
  52.9 22.5 all-gather.7
  77.1 49.9 all-gather.9
  128.6 49.9 all-gather.11
  180.0 49.9 all-gather.13
  255.0 34.0 reduce-scatter.18
  324.7 73.4 reduce-scatter.28
  400.5 97.8 reduce-scatter.24
  500.7 97.8 reduce-scatter.20
  600.8 99.5 reduce-scatter.22
  703.8 24.8 reduce-scatter.30
  732.1 45.9 all-reduce.26
  781.0 25.4 reduce-scatter.26
  809.8 25.4 reduce-scatter.32
  838.0 25.4 reduce-scatter.34
where the time goes:
time: 892 us; the launch traced here: 882 us
  waiting for transfers between devices  517 us (58%)
  blocking collectives  168 us (19%)
  matrix products  81.5 us (9%)
  local copies, waits for them, and re-layouts  42.1 us (5%)
  other arithmetic  41.9 us (5%)
  between operations  18.6 us (2%)
  starting transfers between devices  11.8 us (1%)
    unnamed x20, waiting for transfers between devices  147 us
    reduce_scatter x1, waiting for transfers between devices, reduce_grads(): lax.psum_scatter(grads_all[2], 'fsdp', scatter_dimension=0, tiled=True)  98 us
    reduce_scatter x1, waiting for transfers between devices, reduce_grads(): lax.psum_scatter(grads_all[4], 'fsdp', scatter_dimension=0, tiled=True)  97.9 us
    unnamed x4, blocking collectives  57.6 us
    all_gather x1, waiting for transfers between devices, gather_weights(): lax.all_gather(shards[3], 'fsdp', axis=0, tiled=True)  46.1 us
    all_gather x1, waiting for transfers between devices, gather_weights(): lax.all_gather(shards[4], 'fsdp', axis=0, tiled=True)  44.3 us
    psum x1, blocking collectives, body(): lax.psum((jnp.sum(column * stream_float * stream_float), jnp.sum(column *...  43.7 us
    all_gather x1, waiting for transfers between devices, gather_weights(): lax.all_gather(shards[0], 'fsdp', axis=0, tiled=True)  40.4 us
  transfers between devices with their start and end apart: 18, of which 14 were waited for; matrix products, arithmetic and copies ran while one was open for 16% of the time, Pallas kernels for 0%

commit v1 on v0

v1 whole, which is shorter than its diff:
```python
import jax
import jax.numpy as jnp
from jax import lax
from jax.sharding import PartitionSpec as P

HD = 64


epsilon = 1e-12
rope_base = 1000.0
block_limit = 512
direct_limit = 8


def rope_tables(positions, head_size):
    half_size = head_size // 2
    exponent = jnp.arange(half_size, dtype=jnp.float32) * (2.0 / head_size)
    frequency = jnp.power(jnp.float32(rope_base), -exponent)
    angles = positions[:, None] * frequency[None, :]
    cos_half = jnp.cos(angles)
    sin_half = jnp.sin(angles)
    return (
        jnp.concatenate([cos_half, cos_half], axis=-1),
        jnp.concatenate([sin_half, sin_half], axis=-1),
    )


def rotate(values_in, cos_table, sin_table):
    half_size = values_in.shape[-1] // 2
    turned = jnp.concatenate([-values_in[..., half_size:], values_in[..., :half_size]], axis=-1)
    return values_in * cos_table + turned * sin_table


def unrotate(grads_in, cos_table, sin_table):
    scaled = grads_in * sin_table
    half_size = grads_in.shape[-1] // 2
    turned = jnp.concatenate([scaled[..., half_size:], -scaled[..., :half_size]], axis=-1)
    return grads_in * cos_table + turned


def lookup(table, position):
    marks = jnp.arange(table.shape[0], dtype=jnp.int32) == position
    return jnp.sum(jnp.where(marks, table, 0))


def layer_norm(stream, gain_vec, bias_vec):
    average = jnp.mean(stream, axis=-1, keepdims=True)
    centred = stream - average
    variance = jnp.mean(centred * centred, axis=-1, keepdims=True)
    inverse = lax.rsqrt(variance + epsilon)
    normal = centred * inverse
    return (normal * gain_vec + bias_vec, normal, inverse)


def norm_back(grad_rows, normal, inverse, gain_vec):
    scaled = grad_rows * gain_vec
    first_mean = jnp.mean(scaled, axis=-1, keepdims=True)
    second_mean = jnp.mean(scaled * normal, axis=-1, keepdims=True)
    grad_in = (scaled - first_mean - normal * second_mean) * inverse
    return (grad_in, jnp.sum(grad_rows * normal, axis=0), jnp.sum(grad_rows, axis=0))


def flip(array, axis, mask):
    count = lax.axis_size(axis)
    return lax.ppermute(array, axis, [(i, i ^ mask) for i in range(count)])


def spread(block):
    return [block] + [flip(block, "seq", m) for m in range(1, lax.axis_size("seq"))]


def exchange(blocks):
    return [blocks[0]] + [flip(blocks[m], "seq", m) for m in range(1, len(blocks))]


def unmix(blocks, rank):
    stacked = jnp.stack(blocks)
    for m, block in enumerate(blocks):
        stacked = lax.dynamic_update_index_in_dim(stacked, block, rank ^ m, 0)
    return stacked


def gather_rows(shard):
    count = lax.axis_size("fsdp")
    if count > direct_limit:
        return lax.all_gather(shard, "fsdp", axis=0, tiled=True)
    planes = count // 2
    rank = lax.axis_index("fsdp")
    plane = rank // 2
    blocks = [shard] + [
        lax.ppermute(shard, "fsdp", [(i, (i + 2 * k) % count) for i in range(count)])
        for k in range(1, planes)
    ]
    half = jnp.stack(blocks)
    for k, block in enumerate(blocks):
        half = lax.dynamic_update_index_in_dim(half, block, (plane - k) % planes, 0)
    other = flip(half, "fsdp", 1)
    first = (rank % 2) == 0
    pair = jnp.stack([jnp.where(first, half, other), jnp.where(first, other, half)], axis=1)
    return pair.reshape((count * shard.shape[0],) + shard.shape[1:])


def scatter_rows(grad):
    count = lax.axis_size("fsdp")
    if count > direct_limit:
        return lax.psum_scatter(
            grad.astype(jnp.bfloat16), "fsdp", scatter_dimension=0, tiled=True
        ).astype(jnp.float32)
    planes = count // 2
    rank = lax.axis_index("fsdp")
    plane = rank // 2
    rows = grad.shape[0] // count
    view = grad.reshape(planes, 2, rows, grad.shape[1])
    mine = lax.dynamic_index_in_dim(view, rank % 2, 1, keepdims=False)
    theirs = lax.dynamic_index_in_dim(view, 1 - rank % 2, 1, keepdims=False)
    half = mine + flip(theirs.astype(jnp.bfloat16), "fsdp", 1).astype(jnp.float32)
    low = half.astype(jnp.bfloat16)
    total = lax.dynamic_index_in_dim(half, plane, 0, keepdims=False)
    for k in range(1, planes):
        leaving = lax.dynamic_index_in_dim(low, (plane + k) % planes, 0, keepdims=False)
        total = total + lax.ppermute(
            leaving, "fsdp", [(i, (i + 2 * k) % count) for i in range(count)]
        ).astype(jnp.float32)
    return total


def sum_all(array):
    for axis in ("seq", "fsdp"):
        mask = 1
        while mask < lax.axis_size(axis):
            array = array + flip(array, axis, mask)
            mask *= 2
    return array


def total_of(blocks):
    out = blocks[0].astype(jnp.float32)
    for block in blocks[1:]:
        out = out + block.astype(jnp.float32)
    return out


def masked_scores(query_block, key_rows, key_mask, score_scale):
    scores = (
        jnp.einsum("qhe,khe->hqk", query_block, key_rows, preferred_element_type=jnp.float32)
        * score_scale
    )
    return jnp.where(key_mask[None, None, :], scores, -1e30)


def attend(queries, key_rows, values, key_mask, block_count):
    seqlen, head_count, head_size = queries.shape
    block_rows = min(block_limit, seqlen)
    score_scale = head_size ** (-0.5)

    def one_block(block_index, loop_state):
        out_rows, log_totals = loop_state
        offset = block_index * block_rows
        query_block = lax.dynamic_slice_in_dim(queries, offset, block_rows, 0)
        scores = masked_scores(query_block, key_rows, key_mask, score_scale)
        row_max = jnp.max(scores, axis=-1, keepdims=True)
        raised = jnp.exp(scores - row_max)
        row_total = jnp.sum(raised, axis=-1, keepdims=True)
        attn_probs = (raised / row_total).astype(jnp.bfloat16)
        attended = jnp.einsum(
            "hqk,khe->qhe", attn_probs, values, preferred_element_type=jnp.float32
        )
        attended = attended.astype(jnp.bfloat16).reshape(block_rows, head_count * head_size)
        out_rows = lax.dynamic_update_slice_in_dim(out_rows, attended, offset, 0)
        log_totals = lax.dynamic_update_slice_in_dim(
            log_totals, (row_max + jnp.log(row_total))[..., 0], offset, 1
        )
        return (out_rows, log_totals)

    initial = (
        jnp.zeros((seqlen, head_count * head_size), jnp.bfloat16),
        jnp.zeros((head_count, seqlen), jnp.float32),
    )
    return lax.fori_loop(0, block_count, one_block, initial)


def attend_back(queries, key_rows, values, grad_heads, log_totals, key_mask, block_count):
    seqlen, head_count, head_size = queries.shape
    block_rows = min(block_limit, seqlen)
    score_scale = head_size ** (-0.5)
    grad_shaped = grad_heads.reshape(seqlen, head_count, head_size)

    def one_block(block_index, loop_state):
        grad_query, grad_key, grad_value = loop_state
        offset = block_index * block_rows
        query_block = lax.dynamic_slice_in_dim(queries, offset, block_rows, 0)
        grad_block = lax.dynamic_slice_in_dim(grad_shaped, offset, block_rows, 0)
        log_block = lax.dynamic_slice_in_dim(log_totals, offset, block_rows, 1)
        scores = masked_scores(query_block, key_rows, key_mask, score_scale)
        attn_probs = jnp.exp(scores - log_block[..., None])
        grad_probs = jnp.einsum(
            "qhe,khe->hqk", grad_block, values, preferred_element_type=jnp.float32
        )
        row_dot = jnp.sum(attn_probs * grad_probs, axis=-1, keepdims=True)
        grad_scores = (attn_probs * (grad_probs - row_dot)).astype(jnp.bfloat16)
        query_part = (
            jnp.einsum("hqk,khe->qhe", grad_scores, key_rows, preferred_element_type=jnp.float32)
            * score_scale
        )
        grad_query = lax.dynamic_update_slice_in_dim(
            grad_query, query_part.astype(jnp.bfloat16), offset, 0
        )
        grad_key = (
            grad_key
            + jnp.einsum(
                "hqk,qhe->khe", grad_scores, query_block, preferred_element_type=jnp.float32
            )
            * score_scale
        )
        grad_value = grad_value + jnp.einsum(
            "hqk,qhe->khe",
            attn_probs.astype(jnp.bfloat16),
            grad_block,
            preferred_element_type=jnp.float32,
        )
        return (grad_query, grad_key, grad_value)

    initial = (
        jnp.zeros((seqlen, head_count, head_size), jnp.bfloat16),
        jnp.zeros((seqlen, head_count, head_size), jnp.float32),
        jnp.zeros((seqlen, head_count, head_size), jnp.float32),
    )
    grad_query, grad_key, grad_value = lax.fori_loop(0, block_count, one_block, initial)
    return (grad_query, grad_key.astype(jnp.bfloat16), grad_value.astype(jnp.bfloat16))


def body(
    tokens,
    cotangent,
    w_qkv,
    w_out,
    w_gate,
    w_up,
    w_down,
    gain_one,
    bias_one,
    gain_two,
    bias_two,
    seq_lens,
    slot_seq,
):
    parts = lax.axis_size("seq")
    shards = lax.axis_size("fsdp")
    rank = lax.axis_index("seq")
    owner = lax.axis_index("fsdp")
    rows = tokens.shape[1]
    width = tokens.shape[2]
    shard_rows = w_qkv.shape[0]
    heads = width // HD // parts
    head_width = heads * HD
    hidden = w_down.shape[0]
    piece = hidden // parts
    wide = shards * piece
    seqlen = rows * parts
    stream_in = tokens[0]
    length = lookup(seq_lens, lookup(slot_seq, owner))
    own = jnp.arange(rows, dtype=jnp.int32)
    positions = rank * rows + own
    column = (positions < length).astype(jnp.float32)[:, None]
    block_order = jnp.arange(parts, dtype=jnp.int32) ^ rank
    all_positions = (block_order[:, None] * rows + own[None, :]).reshape(seqlen)
    key_mask = all_positions < length
    block_count = seqlen // min(block_limit, seqlen)

    stream_blocks = spread(stream_in)
    qkv_piece = lax.dynamic_index_in_dim(
        w_qkv.reshape(shard_rows, 3, parts, head_width), rank, 2, keepdims=False
    ).reshape(shard_rows, 3 * head_width)
    full_qkv = gather_rows(qkv_piece)

    def columns_of(weight):
        return lax.dynamic_index_in_dim(
            weight.reshape(shard_rows, shards, parts, piece), rank, 2, keepdims=False
        ).reshape(shard_rows, wide)

    vectors = jnp.concatenate([gain_one, bias_one, gain_two, bias_two])
    vectors = jnp.pad(vectors, (0, width - vectors.shape[0])).reshape(1, width)
    out_piece = jnp.concatenate([w_out, jnp.pad(vectors, ((0, 15), (0, 0)))], axis=0)
    down_piece = lax.dynamic_slice_in_dim(w_down, rank * piece, piece, 0)
    ffn_piece = jnp.concatenate(
        [
            columns_of(w_gate),
            columns_of(w_up),
            down_piece,
        ],
        axis=1,
    )
    out_piece, ffn_piece, full_qkv = lax.optimization_barrier((out_piece, ffn_piece, full_qkv))
    gathered_out = gather_rows(out_piece).reshape(shards, shard_rows + 16, width)
    full_out = gathered_out[:, :shard_rows].reshape(width, width)
    params = gathered_out[:, shard_rows, : 4 * shard_rows].astype(jnp.float32)
    params = params.reshape(shards, 4, shard_rows).transpose(1, 0, 2).reshape(4, width)
    gain_first, bias_first, gain_second, bias_second = (params[i : i + 1] for i in range(4))
    full_ffn = gather_rows(ffn_piece)
    full_gate_up = full_ffn[:, : 2 * wide]
    full_down = full_ffn[:, 2 * wide :]

    stream_all = jnp.concatenate(stream_blocks, axis=0)
    projected = jnp.dot(stream_all, full_qkv, preferred_element_type=jnp.float32).reshape(
        seqlen, 3, heads, HD
    )
    cos_table, sin_table = rope_tables(all_positions.astype(jnp.float32), HD)
    cos_table = cos_table[:, None, :]
    sin_table = sin_table[:, None, :]
    queries = rotate(projected[:, 0], cos_table, sin_table).astype(jnp.bfloat16)
    key_rows = rotate(projected[:, 1], cos_table, sin_table).astype(jnp.bfloat16)
    values = projected[:, 2].astype(jnp.bfloat16)
    head_out, log_totals = attend(queries, key_rows, values, key_mask, block_count)
    mixed = exchange([head_out[m * rows : (m + 1) * rows] for m in range(parts)])
    head_mix = unmix(mixed, rank).transpose(1, 0, 2).reshape(rows, width)
    branch_attn = jnp.dot(head_mix, full_out, preferred_element_type=jnp.float32)
    stream_float = stream_in.astype(jnp.float32)
    normed_float, normal_one, inverse_one = layer_norm(
        stream_float + branch_attn, gain_first, bias_first
    )
    normed_one = normed_float.astype(jnp.bfloat16)
    normed_all = jnp.concatenate(spread(normed_one), axis=0)
    gate_up = jnp.dot(normed_all, full_gate_up, preferred_element_type=jnp.float32)
    gate_proj = gate_up[:, :wide]
    up_proj = gate_up[:, wide:]
    inner_act = (jax.nn.silu(gate_proj) * up_proj).astype(jnp.bfloat16)
    ffn_part = jnp.dot(inner_act, full_down, preferred_element_type=jnp.float32).astype(
        jnp.bfloat16
    )
    branch_ffn = total_of(exchange([ffn_part[m * rows : (m + 1) * rows] for m in range(parts)]))
    out_float, normal_two, inverse_two = layer_norm(
        normed_one.astype(jnp.float32) + branch_ffn, gain_second, bias_second
    )
    layer_out = (out_float * column).astype(jnp.bfloat16)
    grad_rows = cotangent[0].astype(jnp.float32) * column
    grad_two, gain_two_grad, bias_two_grad = norm_back(
        grad_rows, normal_two, inverse_two, gain_second
    )
    grad_ffn = grad_two.astype(jnp.bfloat16)
    grad_ffn_all = jnp.concatenate(spread(grad_ffn), axis=0)
    grad_inner = jnp.einsum("td,fd->tf", grad_ffn_all, full_down, preferred_element_type=jnp.float32)
    sigmoid_gate = jax.nn.sigmoid(gate_proj)
    grad_gate_rows = (
        grad_inner * up_proj * sigmoid_gate * (1.0 + gate_proj * (1.0 - sigmoid_gate))
    ).astype(jnp.bfloat16)
    grad_up_rows = (grad_inner * gate_proj * sigmoid_gate).astype(jnp.bfloat16)
    grad_both = jnp.concatenate([grad_gate_rows, grad_up_rows], axis=1)
    normed_part = jnp.einsum(
        "tf,df->td", grad_both, full_gate_up, preferred_element_type=jnp.float32
    ).astype(jnp.bfloat16)
    grad_normed = (
        total_of(exchange([normed_part[m * rows : (m + 1) * rows] for m in range(parts)])) + grad_two
    )
    down_grad = jnp.einsum("tf,td->fd", inner_act, grad_ffn_all, preferred_element_type=jnp.float32)
    both_grad = jnp.einsum("td,tf->df", normed_all, grad_both, preferred_element_type=jnp.float32)
    ffn_grad = scatter_rows(jnp.concatenate([both_grad, down_grad], axis=1))

    grad_one, gain_one_grad, bias_one_grad = norm_back(
        grad_normed, normal_one, inverse_one, gain_first
    )
    squares = jnp.concatenate(
        [
            jnp.sum(column * stream_float * stream_float, axis=0, keepdims=True),
            jnp.sum(column * branch_attn * branch_attn, axis=0, keepdims=True),
            jnp.sum(column * branch_ffn * branch_ffn, axis=0, keepdims=True),
            gain_one_grad[None],
            bias_one_grad[None],
            gain_two_grad[None],
            bias_two_grad[None],
            jnp.zeros((1, width), jnp.float32),
        ],
        axis=0,
    )
    sums = sum_all(squares)
    denominator = jnp.sum(seq_lens).astype(jnp.float32) * width
    stream_rms = jnp.sqrt(jnp.sum(sums[:3], axis=1) / denominator)
    vector_grads = lax.dynamic_index_in_dim(
        sums[3:7].reshape(4, shards, shard_rows), owner, 1, keepdims=False
    )

    grad_attn = grad_one.astype(jnp.bfloat16)
    grad_mix = (
        jnp.einsum("te,de->td", grad_attn, full_out, preferred_element_type=jnp.float32)
        .astype(jnp.bfloat16)
        .reshape(rows, parts, head_width)
        .transpose(1, 0, 2)
    )
    leaving = [
        lax.dynamic_index_in_dim(grad_mix, rank ^ m, 0, keepdims=False) for m in range(parts)
    ]
    grad_heads = jnp.concatenate(exchange(leaving), axis=0)
    out_grad = scatter_rows(
        jnp.einsum("td,te->de", head_mix, grad_attn, preferred_element_type=jnp.float32)
    )
    grad_query, grad_key, grad_value = attend_back(
        queries, key_rows, values, grad_heads, log_totals, key_mask, block_count
    )
    grad_proj = jnp.stack(
        [
            unrotate(grad_query.astype(jnp.float32), cos_table, sin_table),
            unrotate(grad_key.astype(jnp.float32), cos_table, sin_table),
            grad_value.astype(jnp.float32),
        ],
        axis=1,
    )
    grad_proj = grad_proj.astype(jnp.bfloat16).reshape(seqlen, 3 * head_width)
    token_part = jnp.einsum(
        "tc,dc->td", grad_proj, full_qkv, preferred_element_type=jnp.float32
    ).astype(jnp.bfloat16)
    grad_tokens = (
        total_of(exchange([token_part[m * rows : (m + 1) * rows] for m in range(parts)])) + grad_one
    ).astype(jnp.bfloat16)
    qkv_grad = scatter_rows(
        jnp.einsum("td,tc->dc", stream_all, grad_proj, preferred_element_type=jnp.float32)
    )
    qkv_blocks = unmix(spread(qkv_grad.astype(jnp.bfloat16)), rank).astype(jnp.float32)
    qkv_out = (
        qkv_blocks.reshape(parts, shard_rows, 3, head_width)
        .transpose(1, 2, 0, 3)
        .reshape(shard_rows, 3 * width)
    )
    ffn_blocks = unmix(spread(ffn_grad.astype(jnp.bfloat16)), rank).astype(jnp.float32)

    def restore(blocks):
        return (
            blocks.reshape(parts, shard_rows, shards, piece)
            .transpose(1, 2, 0, 3)
            .reshape(shard_rows, shards * hidden)
        )

    gate_out = restore(ffn_blocks[:, :, :wide])
    up_out = restore(ffn_blocks[:, :, wide : 2 * wide])
    down_out = ffn_blocks[:, :, 2 * wide :].reshape(hidden, width)
    out_split = out_grad.astype(jnp.bfloat16).reshape(parts, shard_rows // parts, width)
    out_sum = total_of(
        exchange(
            [lax.dynamic_index_in_dim(out_split, rank ^ m, 0, keepdims=False) for m in range(parts)]
        )
    )
    out_out = (
        unmix(spread(out_sum.astype(jnp.bfloat16)), rank)
        .astype(jnp.float32)
        .reshape(shard_rows, width)
    )
    return (
        layer_out[None],
        grad_tokens[None],
        qkv_out,
        out_out,
        gate_out,
        up_out,
        down_out,
        vector_grads[0],
        vector_grads[1],
        vector_grads[2],
        vector_grads[3],
        stream_rms,
    )


def solution(mesh):
    placed = (
        P("fsdp", "seq", None),
        P("fsdp", "seq", None),
        P("fsdp", None),
        P("fsdp", None),
        P("fsdp", None),
        P("fsdp", None),
        P("fsdp", None),
        P("fsdp"),
        P("fsdp"),
        P("fsdp"),
        P("fsdp"),
        P(),
        P(),
    )
    return jax.shard_map(
        body,
        mesh=mesh,
        in_specs=placed,
        out_specs=(
            P("fsdp", "seq", None),
            P("fsdp", "seq", None),
            P("fsdp", None),
            P("fsdp", None),
            P("fsdp", None),
            P("fsdp", None),
            P("fsdp", None),
            P("fsdp"),
            P("fsdp"),
            P("fsdp"),
            P("fsdp"),
            P(),
        ),
        check_vma=False,
    )
```

time: 892 us -> 439 us (0.49)
  waiting for transfers between devices: 517 us -> 168 us
  blocking collectives: 168 us -> 0 us
  starting transfers between devices: 11.8 us -> 69.8 us
  local copies, waits for them, and re-layouts: 42.1 us -> 65.5 us
  other arithmetic: 41.9 us -> 59.1 us
  between operations: 18.6 us -> 2.97 us
  matrix products: 81.5 us -> 69.1 us
    reduce_scatter x5 -> x0, waiting for transfers between devices: 212 us -> none  [the longest x1 98 us: reduce_grads(): lax.psum_scatter(grads_all[2], 'fsdp', scatter_dimension=0, tiled=True)]
    ppermute x0 -> x65, waiting for transfers between devices: none -> 168 us  [the longest x47 78.6 us: flip(): return lax.ppermute(array, axis, [(i, i ^ mask) for i in range(count)])]
    unnamed x20 -> x0, waiting for transfers between devices: 147 us -> none
    all_gather x5 -> x0, waiting for transfers between devices: 140 us -> none  [the longest x1 46.1 us: gather_weights(): lax.all_gather(shards[3], 'fsdp', axis=0, tiled=True)]
    ppermute x0 -> x65, starting transfers between devices: none -> 69.8 us  [the longest x47 46 us: flip(): return lax.ppermute(array, axis, [(i, i ^ mask) for i in range(count)])]
    unnamed x4 -> x0, blocking collectives: 57.6 us -> none
    all_gather x5 -> x0, blocking collectives: 49.1 us -> none  [the longest x1 10.2 us: reduce_grads(): lax.all_gather(split[2].astype(jnp.bfloat16), 'seq', axis=0, tiled=True)]
    psum x1 -> x0, blocking collectives: 43.7 us -> none  [body(): lax.psum((jnp.sum(column * stream_float * stream_float), jnp.sum(column *...]
  transfers between devices with their start and end apart: 18 -> 65, of which waited for: 14 -> 33; matrix products, arithmetic and copies ran while one was open for 16% -> 30% of each run, Pallas kernels for 0% -> 0%
where the time goes in v1:
time: 439 us; the launch traced here: 435 us
  waiting for transfers between devices  168 us (38%)
  starting transfers between devices  69.8 us (16%)
  matrix products  69.1 us (16%)
  local copies, waits for them, and re-layouts  65.5 us (15%)
  other arithmetic  59.1 us (13%)
    ppermute x47, waiting for transfers between devices, flip(): return lax.ppermute(array, axis, [(i, i ^ mask) for i in range(count)])  78.6 us
    ppermute x9, waiting for transfers between devices, scatter_rows(): lax.ppermute(leaving, 'fsdp', [(i, (i + 2 * k) % count) for i in range(co...  47.2 us
    ppermute x47, starting transfers between devices, flip(): return lax.ppermute(array, axis, [(i, i ^ mask) for i in range(count)])  46 us
    ppermute x9, waiting for transfers between devices, gather_rows(): lax.ppermute(shard, 'fsdp', [(i, (i + 2 * k) % count) for i in range(coun...  42.4 us
    ppermute x9, starting transfers between devices, gather_rows(): lax.ppermute(shard, 'fsdp', [(i, (i + 2 * k) % count) for i in range(coun...  12.4 us
    ppermute x9, starting transfers between devices, scatter_rows(): lax.ppermute(leaving, 'fsdp', [(i, (i + 2 * k) % count) for i in range(co...  11.4 us
    dot_general x4, matrix products, masked_scores(): jnp.einsum('qhe,khe->hqk', query_block, key_rows, preferred_element_type=...  9.68 us
  transfers between devices with their start and end apart: 65, of which 33 were waited for; matrix products, arithmetic and copies ran while one was open for 30% of the time, Pallas kernels for 0%

profile of v1, /device:TPU:8, one launch (start us, length us, event | category | flops | bytes accessed | tf_op | source)
XLA Modules:
  0.0 435.1 jit_solution(14715432226425273145)
XLA Ops:
  34.2 12.4 %while.34 = (s32[]{:T(128)}, bf16[1024,192]{0,1:T(8,128)(2,1)S(1)}, f32[3,1024]{1,0:T(4,128)S(1)}, bf16[1024,3,64]{0,2,1:T(8,128)(2,1)S(1)}, bf16[1024,3,64]{0,2...) while((s32[]{:T(128)}, bf16[1024,192]{0,1:T(8,128)(2,1)S(1)}, ...), condition=%wide.region_5.6_spmd.clone, body=%wide.region_2.5_spmd.clone.sunk | while | flops 421626368 | bytes 20508868 | solution.py:179
  61.0 5.2 %collective-permute-done.11 = bf16[112,768]{1,0:T(8,128)(2,1)S(1)} collective-permute-done((bf16[112,768]{1,0:T(8,128)(2,1)}, bf16[112,768]{1,0:T(8,128)(2,1)S(1)}, u32[]{:S(2)}, u32[]{:S(2)}) %collective-permute-start.11) | collective-permute-done | bytes 172064 | tf_op jit(solution)/shard_map/ppermute | solution.py:91
  66.2 19.8 %collective-permute-done.12 = bf16[112,768]{1,0:T(8,128)(2,1)S(1)} collective-permute-done((bf16[112,768]{1,0:T(8,128)(2,1)}, bf16[112,768]{1,0:T(8,128)(2,1)S(1)}, u32[]{:S(2)}, u32[]{:S(2)}) %collective-permute-start.12) | collective-permute-done | bytes 172064 | tf_op jit(solution)/shard_map/ppermute | solution.py:91
  88.2 6.4 %collective-permute-done.17 = bf16[96,2304]{1,0:T(8,128)(2,1)S(1)} collective-permute-done((bf16[96,2304]{1,0:T(8,128)(2,1)S(1)}, bf16[96,2304]{1,0:T(8,128)(2,1)S(1)}, u32[]{:S(2)}, u32[]{:S(2)}) %collective-permute-start.17) | collective-permute-done | bytes 442400 | tf_op jit(solution)/shard_map/ppermute | solution.py:91
  94.5 7.6 %collective-permute-done.18 = bf16[96,2304]{1,0:T(8,128)(2,1)S(1)} collective-permute-done((bf16[96,2304]{1,0:T(8,128)(2,1)S(1)}, bf16[96,2304]{1,0:T(8,128)(2,1)S(1)}, u32[]{:S(2)}, u32[]{:S(2)}) %collective-permute-start.18) | collective-permute-done | bytes 442400 | tf_op jit(solution)/shard_map/ppermute | solution.py:91
  119.4 5.9 %collective-permute-done.14 = bf16[256,768]{1,0:T(8,128)(2,1)S(1)} collective-permute-done((bf16[256,768]{1,0:T(8,128)(2,1)S(1)}, bf16[256,768]{1,0:T(8,128)(2,1)S(1)}, u32[]{:S(2)}, u32[]{:S(2)}) %collective-permute-start.14) | collective-permute-done | bytes 393248 | tf_op jit(solution)/shard_map/ppermute | solution.py:65
  125.3 9.2 %collective-permute-done.15 = bf16[256,768]{1,0:T(8,128)(2,1)S(1)} collective-permute-done((bf16[256,768]{1,0:T(8,128)(2,1)S(1)}, bf16[256,768]{1,0:T(8,128)(2,1)S(1)}, u32[]{:S(2)}, u32[]{:S(2)}) %collective-permute-start.15) | collective-permute-done | bytes 393248 | tf_op jit(solution)/shard_map/ppermute | solution.py:65
  148.8 6.7 %collective-permute-done.21 = bf16[256,768]{1,0:T(8,128)(2,1)S(1)} collective-permute-done((bf16[256,768]{1,0:T(8,128)(2,1)}, bf16[256,768]{1,0:T(8,128)(2,1)S(1)}, u32[]{:S(2)}, u32[]{:S(2)}) %collective-permute-start.21) | collective-permute-done | bytes 393248 | tf_op jit(solution)/shard_map/ppermute | solution.py:65
  155.6 8.1 %collective-permute-done.22 = bf16[256,768]{1,0:T(8,128)(2,1)S(1)} collective-permute-done((bf16[256,768]{1,0:T(8,128)(2,1)}, bf16[256,768]{1,0:T(8,128)(2,1)S(1)}, u32[]{:S(2)}, u32[]{:S(2)}) %collective-permute-start.22) | collective-permute-done | bytes 393248 | tf_op jit(solution)/shard_map/ppermute | solution.py:65
  188.3 5.8 %multiply_convert_fusion.2 = (bf16[1024,768]{1,0:T(8,128)(2,1)S(1)}, bf16[1024,768]{1,0:T(8,128)(2,1)S(1)}) fusion(f32[1024,1536]{1,0:T(8,128)} %copy-done.7, bf16[768,2304]{1,0:T(8,128)(2,1)} %bitcast.314, bf16[256,768]{1,0:T(8,128)(2,1)} %collective-permute-done.26, bf16[256,768]{1,0:T(8,128)(2,1)} %collective-permute-done.25, ...), kind=kOutput, calls=%fused_computation.52 | convolution fusion | flops 1224474624 | bytes 12189696 | tf_op jit(solution)/shard_map/td,fd->tf/dot_general | solution.py:341
  210.1 5.6 %collective-permute-done.28 = bf16[256,768]{1,0:T(8,128)(2,1)} collective-permute-done((bf16[256,768]{1,0:T(8,128)(2,1)}, bf16[256,768]{1,0:T(8,128)(2,1)}, u32[]{:S(2)}, u32[]{:S(2)}) %collective-permute-start.28) | collective-permute-done | bytes 393248 | tf_op jit(solution)/shard_map/ppermute | solution.py:65
  237.6 43.0 %while.35 = (s32[]{:T(128)}, bf16[1024,3,64]{0,2,1:T(8,128)(2,1)S(1)}, f32[1024,3,64]{0,2,1:T(8,128)S(1)}, f32[1024,3,64]{0,2,1:T(8,128)}, bf16[1024,3,64]{0,2,1...) while((s32[]{:T(128)}, ...), condition=%wide.region_16.17_spmd.clone, body=%wide.region_14.16_spmd.clone.sunk | while | flops 1031406080 | bytes 96637280 | solution.py:228
  237.8 3.7 fusion.183
  242.9 4.3 multiply_reduce_fusion.7
  263.8 4.3 multiply_reduce_fusion.7
  297.3 6.0 %collective-permute-done.33 = bf16[256,768]{1,0:T(8,128)(2,1)} collective-permute-done((bf16[256,768]{1,0:T(8,128)(2,1)}, bf16[256,768]{1,0:T(8,128)(2,1)}, u32[]{:S(2)}, u32[]{:S(2)}) %collective-permute-start.33) | collective-permute-done | bytes 393248 | tf_op jit(solution)/shard_map/ppermute | solution.py:65
  303.4 7.4 %collective-permute-done.34 = bf16[256,768]{1,0:T(8,128)(2,1)} collective-permute-done((bf16[256,768]{1,0:T(8,128)(2,1)}, bf16[256,768]{1,0:T(8,128)(2,1)}, u32[]{:S(2)}, u32[]{:S(2)}) %collective-permute-start.34) | collective-permute-done | bytes 393248 | tf_op jit(solution)/shard_map/ppermute | solution.py:65
  320.1 4.6 %collective-permute-done.37 = bf16[96,576]{1,0:T(8,128)(2,1)S(1)} collective-permute-done((bf16[96,576]{1,0:T(8,128)(2,1)S(1)}, bf16[96,576]{1,0:T(8,128)(2,1)S(1)}, u32[]{:S(2)}, u32[]{:S(2)}) %collective-permute-start.37) | collective-permute-done | bytes 110624 | tf_op jit(solution)/shard_map/ppermute | solution.py:121
  324.8 7.6 %collective-permute-done.38 = bf16[96,576]{1,0:T(8,128)(2,1)S(1)} collective-permute-done((bf16[96,576]{1,0:T(8,128)(2,1)S(1)}, bf16[96,576]{1,0:T(8,128)(2,1)S(1)}, u32[]{:S(2)}, u32[]{:S(2)}) %collective-permute-start.38) | collective-permute-done | bytes 110624 | tf_op jit(solution)/shard_map/ppermute | solution.py:121
  359.5 4.5 %collective-permute-start.55 = (bf16[96,2304]{1,0:T(8,128)(2,1)S(1)}, bf16[96,2304]{1,0:T(8,128)(2,1)S(1)}, u32[]{:S(2)}, u32[]{:S(2)}) collective-permute-start(bf16[96,2304]{1,0:T(8,128)(2,1)S(1)} %get-tuple-element.462), channel_id=1, source_target_pairs={{0,4},{1,5},{2,6},{3,7},{4,0},{5,1},{6,2},{7,3},{8,12},{9,13},{10,... | collective-permute-start | bytes 1327112 | tf_op jit(solution)/shard_map/ppermute | solution.py:121
  364.0 23.8 %collective-permute-done.54 = bf16[96,2304]{1,0:T(8,128)(2,1)S(1)} collective-permute-done((bf16[96,2304]{1,0:T(8,128)(2,1)S(1)}, bf16[96,2304]{1,0:T(8,128)(2,1)S(1)}, u32[]{:S(2)}, u32[]{:S(2)}) %collective-permute-start.54) | collective-permute-done | bytes 442400 | tf_op jit(solution)/shard_map/ppermute | solution.py:121
  387.8 4.7 %collective-permute-done.55 = bf16[96,2304]{1,0:T(8,128)(2,1)S(1)} collective-permute-done((bf16[96,2304]{1,0:T(8,128)(2,1)S(1)}, bf16[96,2304]{1,0:T(8,128)(2,1)S(1)}, u32[]{:S(2)}, u32[]{:S(2)}) %collective-permute-start.55) | collective-permute-done | bytes 442400 | tf_op jit(solution)/shard_map/ppermute | solution.py:121
  400.3 8.8 %collective-permute-done.57 = bf16[96,2304]{1,0:T(8,128)(2,1)S(1)} collective-permute-done((bf16[96,2304]{1,0:T(8,128)(2,1)S(1)}, bf16[96,2304]{1,0:T(8,128)(2,1)S(1)}, u32[]{:S(2)}, u32[]{:S(2)}) %collective-permute-start.57) | collective-permute-done | bytes 442400 | tf_op jit(solution)/shard_map/ppermute | solution.py:65
  409.1 9.3 %collective-permute-done.58 = bf16[96,2304]{1,0:T(8,128)(2,1)S(1)} collective-permute-done((bf16[96,2304]{1,0:T(8,128)(2,1)S(1)}, bf16[96,2304]{1,0:T(8,128)(2,1)S(1)}, u32[]{:S(2)}, u32[]{:S(2)}) %collective-permute-start.58) | collective-permute-done | bytes 442400 | tf_op jit(solution)/shard_map/ppermute | solution.py:65
  (452 shorter events, 262.3 us)
Async XLA Ops:
  2.9 17.3 %collective-permute-start.3 = (bf16[96,576]{0,1:T(8,128)(2,1)S(1)}, bf16[96,576]{0,1:T(8,128)(2,1)S(1)}, u32[]{:S(2)}, u32[]{:S(2)}) collective-permute-start(bf16[96,576]{0,1:T(8,128)(2,1)S(1)} %bitcast.331), channel_id=1, source_target_pairs={{0,2},{1,3},{2,4},{3,5},{4,6},{5,7},{6,0},{7,1},{8,10},{9,11},{10,... | collective-permute-start | bytes 331784 | tf_op jit(solution)/shard_map/ppermute | solution.py:91
  7.6 21.3 %collective-permute-start = (bf16[256,768]{1,0:T(8,128)(2,1)}, bf16[256,768]{1,0:T(8,128)(2,1)}, u32[]{:S(2)}, u32[]{:S(2)}) collective-permute-start(bf16[256,768]{1,0:T(8,128)(2,1)} %bitcast.316), channel_id=1, source_target_pairs={{0,8},{8,0},{16,24},{24,16},{1,9},{9,1},{17,25},{25,17},{2,10},{10... | collective-permute-start | bytes 1179656 | tf_op jit(solution)/shard_map/ppermute | solution.py:65
  9.1 19.8 %collective-permute-start.1 = (bf16[256,768]{1,0:T(8,128)(2,1)}, bf16[256,768]{1,0:T(8,128)(2,1)}, u32[]{:S(2)}, u32[]{:S(2)}) collective-permute-start(bf16[256,768]{1,0:T(8,128)(2,1)} %bitcast.317), channel_id=1, source_target_pairs={{0,16},{8,24},{16,0},{24,8},{1,17},{9,25},{17,1},{25,9},{2,18},{10... | collective-permute-start | bytes 1179656 | tf_op jit(solution)/shard_map/ppermute | solution.py:65
  53.9 32.2 %collective-permute-start.12 = (bf16[112,768]{1,0:T(8,128)(2,1)}, bf16[112,768]{1,0:T(8,128)(2,1)S(1)}, u32[]{:S(2)}, u32[]{:S(2)}) collective-permute-start(bf16[112,768]{1,0:T(8,128)(2,1)} %fusion.95), channel_id=1, source_target_pairs={{0,6},{1,7},{2,0},{3,1},{4,2},{5,3},{6,4},{7,5},{8,14},{9,15},{10,... | collective-permute-start | bytes 516104 | tf_op jit(solution)/shard_map/ppermute | solution.py:91
  53.9 40.6 %collective-permute-start.17 = (bf16[96,2304]{1,0:T(8,128)(2,1)S(1)}, bf16[96,2304]{1,0:T(8,128)(2,1)S(1)}, u32[]{:S(2)}, u32[]{:S(2)}) collective-permute-start(bf16[96,2304]{1,0:T(8,128)(2,1)S(1)} %pad_maximum_fusion.17), channel_id=1, source_target_pairs={{0,2},{1,3},{2,4},{3,5},{4,6},{5,7},{6,0},{7,1},{8,10},{9,11},{10,... | collective-permute-start | bytes 1327112 | tf_op jit(solution)/shard_map/ppermute | solution.py:91
  55.9 46.2 %collective-permute-start.18 = (bf16[96,2304]{1,0:T(8,128)(2,1)S(1)}, bf16[96,2304]{1,0:T(8,128)(2,1)S(1)}, u32[]{:S(2)}, u32[]{:S(2)}) collective-permute-start(bf16[96,2304]{1,0:T(8,128)(2,1)S(1)} %pad_maximum_fusion.17), channel_id=1, source_target_pairs={{0,4},{1,5},{2,6},{3,7},{4,0},{5,1},{6,2},{7,3},{8,12},{9,13},{10,... | collective-permute-start | bytes 1327112 | tf_op jit(solution)/shard_map/ppermute | solution.py:91
  60.8 43.6 %collective-permute-start.19 = (bf16[96,2304]{1,0:T(8,128)(2,1)S(1)}, bf16[96,2304]{1,0:T(8,128)(2,1)S(1)}, u32[]{:S(2)}, u32[]{:S(2)}) collective-permute-start(bf16[96,2304]{1,0:T(8,128)(2,1)S(1)} %pad_maximum_fusion.17), channel_id=1, source_target_pairs={{0,6},{1,7},{2,0},{3,1},{4,2},{5,3},{6,4},{7,5},{8,14},{9,15},{10,... | collective-permute-start | bytes 1327112 | tf_op jit(solution)/shard_map/ppermute | solution.py:91
  88.1 20.9 %collective-permute-start.13 = (bf16[4,112,768]{2,1,0:T(8,128)(2,1)S(1)}, bf16[4,112,768]{2,1,0:T(8,128)(2,1)S(1)}, u32[]{:S(2)}, u32[]{:S(2)}) collective-permute-start(bf16[4,112,768]{2,1,0:T(8,128)(2,1)S(1)} %constant_dynamic-update-slice_fusion.17), channel_id=1, source_target_pairs={{0,1},{1,0},{2,3},{3,2},{4,5},{5,4},{6,7},{7,6},{8,9},{9,8},{10,11... | collective-permute-start | bytes 2064392 | tf_op jit(solution)/shard_map/ppermute | solution.py:65
  114.8 19.7 %collective-permute-start.15 = (bf16[256,768]{1,0:T(8,128)(2,1)S(1)}, bf16[256,768]{1,0:T(8,128)(2,1)S(1)}, u32[]{:S(2)}, u32[]{:S(2)}) collective-permute-start(bf16[256,768]{1,0:T(8,128)(2,1)S(1)} %add_convert_fusion.1), channel_id=1, source_target_pairs={{0,16},{8,24},{16,0},{24,8},{1,17},{9,25},{17,1},{25,9},{2,18},{10... | collective-permute-start | bytes 1179656 | tf_op jit(solution)/shard_map/ppermute | solution.py:65
  116.4 18.1 %collective-permute-start.16 = (bf16[256,768]{1,0:T(8,128)(2,1)S(1)}, bf16[256,768]{1,0:T(8,128)(2,1)S(1)}, u32[]{:S(2)}, u32[]{:S(2)}) collective-permute-start(bf16[256,768]{1,0:T(8,128)(2,1)S(1)} %add_convert_fusion.1), channel_id=1, source_target_pairs={{0,24},{8,16},{16,8},{24,0},{1,25},{9,17},{17,9},{25,1},{2,26},{10... | collective-permute-start | bytes 1179656 | tf_op jit(solution)/shard_map/ppermute | solution.py:65
  144.6 19.0 %collective-permute-start.22 = (bf16[256,768]{1,0:T(8,128)(2,1)}, bf16[256,768]{1,0:T(8,128)(2,1)S(1)}, u32[]{:S(2)}, u32[]{:S(2)}) collective-permute-start(bf16[256,768]{1,0:T(8,128)(2,1)} %get-tuple-element.471), channel_id=1, source_target_pairs={{0,16},{8,24},{16,0},{24,8},{1,17},{9,25},{17,1},{25,9},{2,18},{10... | collective-permute-start | bytes 1179656 | tf_op jit(solution)/shard_map/ppermute | solution.py:65
  145.4 19.0 %collective-permute-start.23 = (bf16[256,768]{1,0:T(8,128)(2,1)}, bf16[256,768]{1,0:T(8,128)(2,1)}, u32[]{:S(2)}, u32[]{:S(2)}) collective-permute-start(bf16[256,768]{1,0:T(8,128)(2,1)} %get-tuple-element.470), channel_id=1, source_target_pairs={{0,24},{8,16},{16,8},{24,0},{1,25},{9,17},{17,9},{25,1},{2,26},{10... | collective-permute-start | bytes 1179656 | tf_op jit(solution)/shard_map/ppermute | solution.py:65
  170.6 16.8 %collective-permute-start.24 = (bf16[256,768]{1,0:T(8,128)(2,1)}, bf16[256,768]{1,0:T(8,128)(2,1)}, u32[]{:S(2)}, u32[]{:S(2)}) collective-permute-start(bf16[256,768]{1,0:T(8,128)(2,1)} %fusion.119), channel_id=1, source_target_pairs={{0,8},{8,0},{16,24},{24,16},{1,9},{9,1},{17,25},{25,17},{2,10},{10... | collective-permute-start | bytes 1179656 | tf_op jit(solution)/shard_map/ppermute | solution.py:65
  171.1 17.2 %collective-permute-start.25 = (bf16[256,768]{1,0:T(8,128)(2,1)}, bf16[256,768]{1,0:T(8,128)(2,1)}, u32[]{:S(2)}, u32[]{:S(2)}) collective-permute-start(bf16[256,768]{1,0:T(8,128)(2,1)} %fusion.119), channel_id=1, source_target_pairs={{0,16},{8,24},{16,0},{24,8},{1,17},{9,25},{17,1},{25,9},{2,18},{10... | collective-permute-start | bytes 1179656 | tf_op jit(solution)/shard_map/ppermute | solution.py:65
  208.9 146.2 %collective-permute-start.53 = (bf16[4,96,2304]{2,1,0:T(8,128)(2,1)}, bf16[4,96,2304]{2,1,0:T(8,128)(2,1)}, u32[]{:S(2)}, u32[]{:S(2)}) collective-permute-start(bf16[4,96,2304]{2,1,0:T(8,128)(2,1)} %fusion.45), channel_id=1, source_target_pairs={{0,1},{1,0},{2,3},{3,2},{4,5},{5,4},{6,7},{7,6},{8,9},{9,8},{10,11... | collective-permute-start | bytes 5308424 | tf_op jit(solution)/shard_map/ppermute | solution.py:65
  236.5 52.4 %collective-permute-start.63 = (f32[8,768]{1,0:T(8,128)}, f32[8,768]{1,0:T(8,128)}, u32[]{:S(2)}, u32[]{:S(2)}) collective-permute-start(f32[8,768]{1,0:T(8,128)} %add.515), channel_id=1, source_target_pairs={{0,2},{1,3},{2,0},{3,1},{4,6},{5,7},{6,4},{7,5},{8,10},{9,11},{10,... | collective-permute-start | bytes 73736 | tf_op jit(solution)/shard_map/ppermute | solution.py:65
  286.9 26.1 %collective-permute-start.36 = (bf16[4,96,576]{2,1,0:T(8,128)(2,1)}, bf16[4,96,576]{2,1,0:T(8,128)(2,1)}, u32[]{:S(2)}, u32[]{:S(2)}) collective-permute-start(bf16[4,96,576]{2,1,0:T(8,128)(2,1)} %fusion.77), channel_id=1, source_target_pairs={{0,1},{1,0},{2,3},{3,2},{4,5},{5,4},{6,7},{7,6},{8,9},{9,8},{10,11... | collective-permute-start | bytes 1327112 | tf_op jit(solution)/shard_map/ppermute | solution.py:65
  291.5 19.2 %collective-permute-start.34 = (bf16[256,768]{1,0:T(8,128)(2,1)}, bf16[256,768]{1,0:T(8,128)(2,1)}, u32[]{:S(2)}, u32[]{:S(2)}) collective-permute-start(bf16[256,768]{1,0:T(8,128)(2,1)} %get-tuple-element.465), channel_id=1, source_target_pairs={{0,16},{8,24},{16,0},{24,8},{1,17},{9,25},{17,1},{25,9},{2,18},{10... | collective-permute-start | bytes 1179656 | tf_op jit(solution)/shard_map/ppermute | solution.py:65
  319.1 16.7 %collective-permute-start.44 = (bf16[96,768]{1,0:T(8,128)(2,1)S(1)}, bf16[96,768]{1,0:T(8,128)(2,1)S(1)}, u32[]{:S(2)}, u32[]{:S(2)}) collective-permute-start(bf16[96,768]{1,0:T(8,128)(2,1)S(1)} %get-tuple-element.485), channel_id=1, source_target_pairs={{0,2},{1,3},{2,4},{3,5},{4,6},{5,7},{6,0},{7,1},{8,10},{9,11},{10,... | collective-permute-start | bytes 442376 | tf_op jit(solution)/shard_map/ppermute | solution.py:121
  358.2 29.6 %collective-permute-start.54 = (bf16[96,2304]{1,0:T(8,128)(2,1)S(1)}, bf16[96,2304]{1,0:T(8,128)(2,1)S(1)}, u32[]{:S(2)}, u32[]{:S(2)}) collective-permute-start(bf16[96,2304]{1,0:T(8,128)(2,1)S(1)} %get-tuple-element.460), channel_id=1, source_target_pairs={{0,2},{1,3},{2,4},{3,5},{4,6},{5,7},{6,0},{7,1},{8,10},{9,11},{10,... | collective-permute-start | bytes 1327112 | tf_op jit(solution)/shard_map/ppermute | solution.py:121
  359.5 33.0 %collective-permute-start.55 = (bf16[96,2304]{1,0:T(8,128)(2,1)S(1)}, bf16[96,2304]{1,0:T(8,128)(2,1)S(1)}, u32[]{:S(2)}, u32[]{:S(2)}) collective-permute-start(bf16[96,2304]{1,0:T(8,128)(2,1)S(1)} %get-tuple-element.462), channel_id=1, source_target_pairs={{0,4},{1,5},{2,6},{3,7},{4,0},{5,1},{6,2},{7,3},{8,12},{9,13},{10,... | collective-permute-start | bytes 1327112 | tf_op jit(solution)/shard_map/ppermute | solution.py:121
  364.0 31.8 %collective-permute-start.56 = (bf16[96,2304]{1,0:T(8,128)(2,1)S(1)}, bf16[96,2304]{1,0:T(8,128)(2,1)S(1)}, u32[]{:S(2)}, u32[]{:S(2)}) collective-permute-start(bf16[96,2304]{1,0:T(8,128)(2,1)S(1)} %get-tuple-element.461), channel_id=1, source_target_pairs={{0,6},{1,7},{2,0},{3,1},{4,2},{5,3},{6,4},{7,5},{8,14},{9,15},{10,... | collective-permute-start | bytes 1327112 | tf_op jit(solution)/shard_map/ppermute | solution.py:121
  397.4 21.0 %collective-permute-start.58 = (bf16[96,2304]{1,0:T(8,128)(2,1)S(1)}, bf16[96,2304]{1,0:T(8,128)(2,1)S(1)}, u32[]{:S(2)}, u32[]{:S(2)}) collective-permute-start(bf16[96,2304]{1,0:T(8,128)(2,1)S(1)} %fusion.54), channel_id=1, source_target_pairs={{0,16},{8,24},{16,0},{24,8},{1,17},{9,25},{17,1},{25,9},{2,18},{10... | collective-permute-start | bytes 1327112 | tf_op jit(solution)/shard_map/ppermute | solution.py:65
  398.0 20.4 %collective-permute-start.59 = (bf16[96,2304]{1,0:T(8,128)(2,1)S(1)}, bf16[96,2304]{1,0:T(8,128)(2,1)S(1)}, u32[]{:S(2)}, u32[]{:S(2)}) collective-permute-start(bf16[96,2304]{1,0:T(8,128)(2,1)S(1)} %fusion.54), channel_id=1, source_target_pairs={{0,24},{8,16},{16,8},{24,0},{1,25},{9,17},{17,9},{25,1},{2,26},{10... | collective-permute-start | bytes 1327112 | tf_op jit(solution)/shard_map/ppermute | solution.py:65
  (109 other events, 921.4 us)
